TPU v7x, 128 devices: a whole 4x4x4 slice. The times are simulated.
128 devices in a mesh: seq: 16 (over z_lo, y, core), head: 8 (over x, z_hi).
Axes of the slice: x: 4, y: 4, z: 4 (z_hi: 2, z_lo: 2; z = z_hi * 2 + z_lo), core: 2. Of those that a mesh axis runs over, the one named last changes fastest.
Arguments:
- frames: bfloat16 [8192, 2048], P('seq')
- w_query: bfloat16 [2048, 2048], P(None, 'head'), may hold values from -0.125 to 0.125
- w_key: bfloat16 [2048, 2048], P(None, 'head'), may hold values from -0.125 to 0.125
- w_value: bfloat16 [2048, 2048], P(None, 'head'), may hold values from -0.125 to 0.125
- w_out: bfloat16 [2048, 2048], P('head'), may hold values from -1 to 1
- conv_taps: float32 [31, 2048], P(None, 'head'), may hold values from -1 to 1
- conv_bias: float32 [2048], P('head'), may hold values from -1 to 1
- norm_gain: float32 [2048], replicated, may hold values from 0.5 to 1.5
- w_up: bfloat16 [2048, 8192], P(None, 'head'), may hold values from -0.125 to 0.125
- w_down: bfloat16 [8192, 2048], P('head'), may hold values from -0.0625 to 0.0625
- block_lists: int32 [64, 8], P('seq'), may hold values from 0 to 63, as said below
- block_counts: int32 [64], P('seq'), may hold values from 1 to 8, as said below
Outputs:
- layer_out: bfloat16 [8192, 2048], P('seq', 'head')
Inputs may be any that keep to these rules, and one draw needn't show every extreme that they name: `block_lists`: entry 0 of query block b's list is b itself; the 8 entries of a list are distinct block indices. `block_counts`: query block 0 has all 8 entries active.
All inputs are finite; a program needn't handle non-finite values.
Results may differ from a plain program's by a relative error of at most 0.02.
The roundings to bfloat16 on the way count: a program that leaves them out, or rounds other values in their place, can miss the bound.
Values may be sent and summed in bfloat16 or wider, within the bound.
A program may use at most 128 MiB of HBM per device.

v0:
```python
import math
import jax
import jax.numpy as jnp
from jax import lax
from jax.sharding import PartitionSpec as P

HD = 64
KERNEL = 31


def extended(cells, sides, width):
    for axis, dim in sides:
        count = lax.axis_size(axis)
        ends = count - 1
        head = lax.slice_in_dim(cells, 0, width, axis=dim)
        tail = lax.slice_in_dim(cells, cells.shape[dim] - width, cells.shape[dim], axis=dim)
        cells = jnp.concatenate(
            [
                lax.ppermute(tail, axis, [(i, (i + 1) % count) for i in range(ends)]),
                cells,
                lax.ppermute(head, axis, [((i + 1) % count, i) for i in range(ends)]),
            ],
            axis=dim,
        )
    return cells


def on_device(
    frames,
    w_query,
    w_key,
    w_value,
    w_out,
    conv_taps,
    conv_bias,
    norm_gain,
    w_up,
    w_down,
    block_lists,
    block_counts,
):
    frame_rows = frames.shape[0]
    width_dev = w_query.shape[1]
    heads_dev = width_dev // HD
    query_blocks = block_lists.shape[0]
    block_rows = frame_rows // query_blocks
    total_blocks = query_blocks * lax.axis_size("seq")
    query = jnp.dot(frames, w_query, preferred_element_type=jnp.float32).astype(jnp.bfloat16)
    keys = jnp.dot(frames, w_key, preferred_element_type=jnp.float32).astype(jnp.bfloat16)
    values = jnp.dot(frames, w_value, preferred_element_type=jnp.float32).astype(jnp.bfloat16)
    slot_live = jnp.arange(block_lists.shape[1])[None, :] < block_counts[:, None]
    hits = (block_lists[:, :, None] == jnp.arange(total_blocks)[None, None, :]) & slot_live[
        :, :, None
    ]
    table = jnp.sum(hits.astype(jnp.float32), axis=1)
    query_heads = query.reshape(frame_rows, heads_dev, HD)
    stacked = jnp.stack([keys, values])

    def allowed_of(key_start, count):
        key_block = (key_start + jnp.arange(count)) // block_rows
        onehot = (key_block[:, None] == jnp.arange(total_blocks)[None, :]).astype(jnp.float32)
        coarse = jnp.dot(table, onehot.T)
        return jnp.repeat(coarse, block_rows, axis=0) > 0.5

    def update(carry, key_part, value_part, allowed):
        run_max, run_sum, run_acc = carry
        count = key_part.shape[0]
        key_heads = key_part.reshape(count, heads_dev, HD)
        value_heads = value_part.reshape(count, heads_dev, HD)
        scores = (
            jnp.einsum("qhd,khd->hqk", query_heads, key_heads, preferred_element_type=jnp.float32)
            * 0.125
        )
        scores = jnp.where(allowed[None], scores, -1e30)
        new_max = jnp.maximum(run_max, jnp.max(scores, axis=2))
        probs = jnp.where(allowed[None], jnp.exp(scores - new_max[:, :, None]), 0.0)
        rescale = jnp.exp(run_max - new_max)
        new_sum = run_sum * rescale + jnp.sum(probs, axis=2)
        new_acc = run_acc * rescale[:, :, None] + jnp.einsum(
            "hqk,khd->hqd",
            probs.astype(jnp.bfloat16),
            value_heads,
            preferred_element_type=jnp.float32,
        )
        return (new_max, new_sum, new_acc)

    start_state = (
        jnp.full((heads_dev, frame_rows), -1e30, jnp.float32),
        jnp.zeros((heads_dev, frame_rows), jnp.float32),
        jnp.zeros((heads_dev, frame_rows, HD), jnp.float32),
    )
    carry = start_state
    piece = lax.all_gather(stacked, "seq", axis=1, tiled=True)
    count = piece.shape[1]
    step_rows = math.gcd(count, 512)
    turns = count // step_rows
    parts = piece.reshape(2, turns, step_rows, width_dev).swapaxes(0, 1)
    offsets = step_rows * jnp.arange(turns)

    def visit(inner, item):
        part, offset = item
        allowed = allowed_of(offset, step_rows)
        inner = update(inner, part[0], part[1], allowed)
        return (inner, None)

    carry, _ = lax.scan(visit, carry, (parts, offsets))
    run_max, run_sum, run_acc = carry
    attended = (
        (run_acc / run_sum[:, :, None])
        .transpose(1, 0, 2)
        .reshape(frame_rows, width_dev)
        .astype(jnp.bfloat16)
    )
    columns = w_out
    mixed = lax.psum_scatter(
        jnp.einsum("fk,kc->cf", attended, columns, preferred_element_type=jnp.float32).astype(
            jnp.bfloat16
        ),
        "head",
        scatter_dimension=0,
        tiled=True,
    ).astype(jnp.float32)
    own_start = lax.axis_index("head") * width_dev
    residual_in = lax.dynamic_slice_in_dim(frames, own_start, width_dev, 1).T.astype(jnp.float32)
    stream = (residual_in + mixed).astype(jnp.bfloat16)
    padded = extended(stream, (("seq", 1),), KERNEL // 2).astype(jnp.float32)
    conv_sum = jnp.zeros((width_dev, frame_rows), jnp.float32)
    for tap in range(KERNEL):
        conv_sum = conv_sum + conv_taps[tap][:, None] * padded[:, tap : tap + frame_rows]
    second = (stream.astype(jnp.float32) + jax.nn.silu(conv_sum + conv_bias[:, None])).astype(
        jnp.bfloat16
    )
    whole = lax.all_gather(second, "head", axis=0, tiled=True).astype(jnp.float32)
    mean = jnp.mean(whole, axis=0, keepdims=True)
    centered = whole - mean
    var = jnp.mean(centered * centered, axis=0, keepdims=True)
    normed = (centered * lax.rsqrt(var + 1e-05) * norm_gain[:, None]).astype(jnp.bfloat16)
    upper = jnp.einsum("df,dk->fk", normed, w_up, preferred_element_type=jnp.float32)
    hidden = jax.nn.silu(upper).astype(jnp.bfloat16)
    columns = w_down
    ffsum = lax.psum_scatter(
        jnp.einsum("fk,kc->cf", hidden, columns, preferred_element_type=jnp.float32).astype(
            jnp.bfloat16
        ),
        "head",
        scatter_dimension=0,
        tiled=True,
    ).astype(jnp.float32)
    return (second.astype(jnp.float32) + ffsum).astype(jnp.bfloat16).T


def solution(mesh):
    placed = (
        P("seq", None),
        P(None, "head"),
        P(None, "head"),
        P(None, "head"),
        P("head", None),
        P(None, "head"),
        P("head"),
        P(),
        P(None, "head"),
        P("head", None),
        P("seq", None),
        P("seq"),
    )
    return jax.shard_map(
        on_device, mesh=mesh, in_specs=placed, out_specs=P("seq", "head"), check_vma=False
    )
```

profile of v0, /device:TPU:0, one launch (start us, length us, event | category | flops | bytes accessed | tf_op | source)
XLA Modules:
  0.0 521.4 jit_solution(5680154871138046375)
XLA Ops:
  6.6 2.7 fusion.32
  9.3 2.6 fusion.33
  13.0 2.3 convolution_convert_fusion.2
  15.4 52.2 %all-gather.3.cloned.1.call-done = bf16[2,8192,256]{2,1,0:T(8,128)(2,1)} async-done(((bf16[2,512,256]{2,1,0:T(8,128)(2,1)}), bf16[2,8192,256]{2,1,0:T(8,128)(2,1)}) %all-gather.3.cloned.1.call-update) | async-done | bytes 8388624 | tf_op jit(solution)/shard_map/all_gather | solution.py:93
  67.5 12.3 %copy.18 = bf16[2,16,512,256]{2,3,0,1:T(8,128)(2,1)} copy(bf16[2,16,512,256]{3,2,1,0:T(8,128)(2,1)} %bitcast.121) | data formatting | bytes 16777216 | tf_op jit(solution)/shard_map/reshape | solution.py:97
  79.9 196.1 %while.17 = (s32[]{:T(128)}, f32[4,512]{1,0:T(4,128)S(1)}, f32[4,512]{1,0:T(4,128)S(1)}, f32[4,512,64]{1,2,0:T(8,128)S(1)}, s32[16]{0:T(128)S(1)}, /*index=5*/bf...) while((s32[]{:T(128)}, f32[4,512]{1,0:T(4,128)S(1)}, ...), condition=%wide.region_4.5_spmd.clone, body=%wide.region_1.4_spmd.clone.sunk | while | flops 282775552 | bytes 33960632 | solution.py:106
  81.6 1.6 broadcast_in_dim.102
  84.4 2.9 fusion.104
  87.3 3.4 fusion.105
  93.8 1.6 broadcast_in_dim.102
  96.7 2.9 fusion.104
  99.5 3.4 fusion.105
  106.1 1.6 broadcast_in_dim.102
  108.9 2.9 fusion.104
  111.8 3.4 fusion.105
  118.3 1.6 broadcast_in_dim.102
  121.2 2.9 fusion.104
  124.0 3.4 fusion.105
  130.6 1.6 broadcast_in_dim.102
  133.4 2.9 fusion.104
  136.3 3.4 fusion.105
  142.9 1.6 broadcast_in_dim.102
  145.7 2.9 fusion.104
  148.6 3.4 fusion.105
  155.1 1.6 broadcast_in_dim.102
  157.9 2.9 fusion.104
  160.8 3.4 fusion.105
  167.4 1.6 broadcast_in_dim.102
  170.2 2.9 fusion.104
  173.1 3.4 fusion.105
  179.6 1.6 broadcast_in_dim.102
  182.4 2.9 fusion.104
  185.3 3.4 fusion.105
  191.9 1.6 broadcast_in_dim.102
  194.7 2.9 fusion.104
  197.6 3.4 fusion.105
  204.1 1.6 broadcast_in_dim.102
  207.0 2.9 fusion.104
  209.8 3.4 fusion.105
  216.4 1.6 broadcast_in_dim.102
  219.2 2.9 fusion.104
  222.1 3.4 fusion.105
  228.6 1.6 broadcast_in_dim.102
  231.5 2.9 fusion.104
  234.3 3.4 fusion.105
  240.9 1.6 broadcast_in_dim.102
  243.7 2.9 fusion.104
  246.6 3.4 fusion.105
  253.1 1.6 broadcast_in_dim.102
  256.0 2.9 fusion.104
  258.8 3.4 fusion.105
  265.4 1.6 broadcast_in_dim.102
  268.2 2.9 fusion.104
  271.1 3.4 fusion.105
  276.0 2.1 fusion.23
  278.2 76.4 %reduce-scatter.3.cloned.1.call-done = bf16[256,512]{0,1:T(8,128)(2,1)} async-done(((bf16[2048,512]{0,1:T(8,128)(2,1)}), bf16[256,512]{0,1:T(8,128)(2,1)}) %reduce-scatter.3.cloned.1.call-update) | async-done | bytes 262160 | tf_op jit(solution)/shard_map/reduce_scatter | solution.py:115
  358.4 3.5 collective-permute-done.1
  361.9 2.9 add_convert_fusion.1
  365.1 59.7 %all-gather.5.cloned.1.call-done = bf16[2048,512]{0,1:T(8,128)(2,1)} async-done(((bf16[256,512]{0,1:T(8,128)(2,1)}), bf16[2048,512]{0,1:T(8,128)(2,1)}) %all-gather.5.cloned.1.call-update) | async-done | bytes 2097168 | tf_op jit(solution)/shard_map/all_gather | solution.py:133
  424.8 2.1 convert_reduce_fusion
  426.9 2.3 fusion.20
  429.2 9.6 %fusion.24 = bf16[2048,512]{0,1:T(8,128)(2,1)} fusion(bf16[1024,2048]{1,0:T(8,128)(2,1)} %param.23, bf16[2048,1024]{1,0:T(8,128)(2,1)} %param.22, bf16[2048,512]{0,1:T(8,128)(2,1)S(1)} %copy-done.2, f32[2048]{0:T(1024)S(1)} %copy-done.8, f32[512]{0:T(512)S(1)} %add_rsqrt_fusion, f32[512]{0:T(512)S(1)} %broadcast_multiply_fusion), kind=kOutput, calls=%fused_computation.42 | convolution fusion | flops 4303880192 | bytes 12595200 | tf_op jit(solution)/shard_map/fk,kc->cf/dot_general | solution.py:142
  438.9 74.3 %reduce-scatter.5.cloned.1.call-done = bf16[256,512]{0,1:T(8,128)(2,1)} async-done(((bf16[2048,512]{0,1:T(8,128)(2,1)}), bf16[256,512]{0,1:T(8,128)(2,1)}) %reduce-scatter.5.cloned.1.call-update) | async-done | bytes 262160 | tf_op jit(solution)/shard_map/reduce_scatter | solution.py:141
  513.1 1.7 fusion.68
  (236 shorter events, 74.7 us)
Async XLA Ops:
  6.5 269.5 %copy-start = (bf16[256,2048]{1,0:T(8,128)(2,1)S(1)}, bf16[256,2048]{1,0:T(8,128)(2,1)}, u32[]{:S(2)}) copy-start(bf16[256,2048]{1,0:T(8,128)(2,1)} %param.18) | copy-start | bytes 3145732
  6.5 6.3 %copy-start.9 = (s32[4]{0:T(128)S(1)}, s32[4]{0:T(128)}, u32[]{:S(2)}) copy-start(s32[4]{0:T(128)} %param.25) | copy-start | bytes 52
  6.5 6.4 %copy-start.5 = (s32[4,8]{1,0:T(4,128)S(1)}, s32[4,8]{1,0:T(4,128)}, u32[]{:S(2)}) copy-start(s32[4,8]{1,0:T(4,128)} %param.24) | copy-start | bytes 388
  6.5 6.5 %copy-start.7 = (bf16[2048,256]{1,0:T(8,128)(2,1)S(1)}, bf16[2048,256]{1,0:T(8,128)(2,1)}, u32[]{:S(2)}) copy-start(bf16[2048,256]{1,0:T(8,128)(2,1)} %param.15) | copy-start | bytes 3145732
  6.5 61.0 %all-gather.3.cloned.1.call-start = ((), (), s32[]{:S(2)}) async-start(), calls=%async_computation.2 | async-start | bytes 8912896 | tf_op jit(solution)/shard_map/all_gather | solution.py:93
  12.7 341.9 %reduce-scatter.3.cloned.1.call-start = ((), (), s32[]{:S(2)}) async-start(), calls=%async_computation.3 | async-start | bytes 2359296 | tf_op jit(solution)/shard_map/reduce_scatter | solution.py:115
  87.3 3.4 copy-start.1
  99.5 3.4 copy-start.1
  111.8 3.4 copy-start.1
  124.0 3.4 copy-start.1
  136.3 3.4 copy-start.1
  148.5 3.4 copy-start.1
  160.8 3.4 copy-start.1
  173.1 3.4 copy-start.1
  185.3 3.4 copy-start.1
  197.6 3.4 copy-start.1
  209.8 3.4 copy-start.1
  222.1 3.4 copy-start.1
  234.3 3.4 copy-start.1
  246.6 3.4 copy-start.1
  258.8 3.4 copy-start.1
  271.1 3.4 copy-start.1
  275.9 2.3 copy-start.4
  276.0 85.9 %copy-start.6 = (f32[256]{0:T(256)S(1)}, f32[256]{0:T(256)}, u32[]{:S(2)}) copy-start(f32[256]{0:T(256)} %param.20) | copy-start | bytes 3076
  278.1 146.7 %all-gather.5.cloned.1.call-start = ((), (), s32[]{:S(2)}) async-start(), calls=%async_computation.4 | async-start | bytes 2359296 | tf_op jit(solution)/shard_map/all_gather | solution.py:133
  355.7 2.6 collective-permute-start
  357.0 4.8 collective-permute-start.1
  364.8 64.4 %copy-start.8 = (f32[2048]{0:T(1024)S(1)}, f32[2048]{0:T(1024)}, u32[]{:S(2)}) copy-start(f32[2048]{0:T(1024)} %param.21) | copy-start | bytes 24580
  364.9 148.2 %reduce-scatter.5.cloned.1.call-start = ((), (), s32[]{:S(2)}) async-start(), calls=%async_computation.5 | async-start | bytes 2359296 | tf_op jit(solution)/shard_map/reduce_scatter | solution.py:141
  424.8 4.4 copy-start.2
  429.2 83.9 %copy-start.3 = (bf16[256,512]{0,1:T(8,128)(2,1)S(1)}, bf16[256,512]{0,1:T(8,128)(2,1)}, u32[]{:S(2)}) copy-start(bf16[256,512]{0,1:T(8,128)(2,1)} %add_convert_fusion.1) | copy-start | bytes 786436
Sparse Core Ops, SparseCore 0:
  12.9 54.6 all-gather.2
  278.2 76.3 reduce-scatter.2
  365.0 59.8 all-gather.4
  439.0 74.0 reduce-scatter.4
where the time goes:
time: 522 us; the launch traced here: 521 us
  waiting for transfers between devices  266 us (51%)
  matrix products  90.8 us (17%)
  other arithmetic  75.9 us (15%)
  local copies, waits for them, and re-layouts  71.2 us (14%)
  between operations  13.3 us (3%)
    reduce_scatter x1, waiting for transfers between devices, on_device(): lax.psum_scatter(jnp.einsum('fk,kc->cf', attended, columns, preferred_ele...  76.4 us
    reduce_scatter x1, waiting for transfers between devices, on_device(): lax.psum_scatter(jnp.einsum('fk,kc->cf', hidden, columns, preferred_eleme...  74.3 us
    all_gather x1, waiting for transfers between devices, on_device(): lax.all_gather(second, 'head', axis=0, tiled=True).astype(jnp.float32)  59.7 us
    reduce_sum x16, other arithmetic, update(): new_sum = run_sum * rescale + jnp.sum(probs, axis=2)  54.2 us
    all_gather x1, waiting for transfers between devices, on_device(): piece = lax.all_gather(stacked, 'seq', axis=1, tiled=True)  52.2 us
    dot_general x16, matrix products, update(): jnp.einsum('qhd,khd->hqk', query_heads, key_heads, preferred_element_type...  45.9 us
    broadcast_in_dim x16, local copies, waits for them, and re-layouts, allowed_of(): return jnp.repeat(coarse, block_rows, axis=0) > 0.5  25.6 us
    dot_general x16, matrix products, update(): jnp.einsum('hqk,khd->hqd', probs.astype(jnp.bfloat16), value_heads, prefe...  21.6 us
  transfers between devices with their start and end apart: 6, of which 5 were waited for; matrix products, arithmetic and copies ran while one was open for 0% of the time, Pallas kernels for 0%

commit v1 on v0

--- a/solution.py
+++ b/solution.py
@@ -130,7 +130,9 @@
     second = (stream.astype(jnp.float32) + jax.nn.silu(conv_sum + conv_bias[:, None])).astype(
         jnp.bfloat16
     )
-    whole = lax.all_gather(second, "head", axis=0, tiled=True).astype(jnp.float32)
+    whole = jnp.concatenate(
+        lax.all_to_all(jnp.stack([second] * lax.axis_size("head")), "head", 0, 0), axis=0
+    ).astype(jnp.float32)
     mean = jnp.mean(whole, axis=0, keepdims=True)
     centered = whole - mean
     var = jnp.mean(centered * centered, axis=0, keepdims=True)

time: 522 us -> 493 us (0.944)
  waiting for transfers between devices: 266 us -> 208 us
  blocking collectives: 0 us -> 31.3 us
    all_gather x1 -> x0, waiting for transfers between devices: 59.7 us -> none  [on_device(): lax.all_gather(second, 'head', axis=0, tiled=True).astype(jnp.float32)]
    all_to_all x0 -> x1, blocking collectives: none -> 31.3 us  [on_device(): lax.all_to_all(jnp.stack([second] * lax.axis_size('head')), 'head', 0, 0)]
  transfers between devices with their start and end apart: 6 -> 5, of which waited for: 5 -> 4; matrix products, arithmetic and copies ran while one was open for 0% -> 1% of each run, Pallas kernels for 0% -> 0%
where the time goes in v1:
time: 493 us; the launch traced here: 492 us
  waiting for transfers between devices  208 us (42%)
  matrix products  90.9 us (18%)
  other arithmetic  72.5 us (15%)
  local copies, waits for them, and re-layouts  71.6 us (15%)
  blocking collectives  31.3 us (6%)
  between operations  13.3 us (3%)
    reduce_scatter x1, waiting for transfers between devices, on_device(): lax.psum_scatter(jnp.einsum('fk,kc->cf', attended, columns, preferred_ele...  76.4 us
    reduce_scatter x1, waiting for transfers between devices, on_device(): lax.psum_scatter(jnp.einsum('fk,kc->cf', hidden, columns, preferred_eleme...  76.2 us
    reduce_sum x16, other arithmetic, update(): new_sum = run_sum * rescale + jnp.sum(probs, axis=2)  54.2 us
    all_gather x1, waiting for transfers between devices, on_device(): piece = lax.all_gather(stacked, 'seq', axis=1, tiled=True)  52.2 us
    dot_general x16, matrix products, update(): jnp.einsum('qhd,khd->hqk', query_heads, key_heads, preferred_element_type...  45.7 us
    all_to_all x1, blocking collectives, on_device(): lax.all_to_all(jnp.stack([second] * lax.axis_size('head')), 'head', 0, 0)  31.3 us
    broadcast_in_dim x16, local copies, waits for them, and re-layouts, allowed_of(): return jnp.repeat(coarse, block_rows, axis=0) > 0.5  25.6 us
    dot_general x16, matrix products, update(): jnp.einsum('hqk,khd->hqd', probs.astype(jnp.bfloat16), value_heads, prefe...  21.9 us
  transfers between devices with their start and end apart: 5, of which 4 were waited for; matrix products, arithmetic and copies ran while one was open for 1% of the time, Pallas kernels for 0%

profile of v1, /device:TPU:0, one launch (start us, length us, event | category | flops | bytes accessed | tf_op | source)
XLA Modules:
  0.0 491.6 jit_solution(12425076827189549539)
XLA Ops:
  6.6 2.7 fusion.23
  9.3 2.6 fusion.24
  13.0 2.4 convolution_convert_fusion.2
  15.4 52.2 %all-gather.2.cloned.1.call-done = bf16[2,8192,256]{2,1,0:T(8,128)(2,1)} async-done(((bf16[2,512,256]{2,1,0:T(8,128)(2,1)}), bf16[2,8192,256]{2,1,0:T(8,128)(2,1)}) %all-gather.2.cloned.1.call-update) | async-done | bytes 8388624 | tf_op jit(solution)/shard_map/all_gather | solution.py:93
  67.5 12.3 %copy.19 = bf16[2,16,512,256]{2,3,0,1:T(8,128)(2,1)} copy(bf16[2,16,512,256]{3,2,1,0:T(8,128)(2,1)} %bitcast.130) | data formatting | bytes 16777216 | tf_op jit(solution)/shard_map/reshape | solution.py:97
  79.8 196.2 %while.17 = (s32[]{:T(128)}, f32[4,512]{1,0:T(4,128)S(1)}, f32[4,512]{1,0:T(4,128)S(1)}, f32[4,512,64]{1,2,0:T(8,128)S(1)}, s32[16]{0:T(128)S(1)}, /*index=5*/bf...) while((s32[]{:T(128)}, f32[4,512]{1,0:T(4,128)S(1)}, ...), condition=%wide.region_4.5_spmd.clone, body=%wide.region_1.4_spmd.clone.sunk | while | flops 282775552 | bytes 33960632 | solution.py:106
  81.6 1.6 broadcast_in_dim.102
  84.4 2.9 fusion.97
  87.3 3.4 fusion.98
  93.8 1.6 broadcast_in_dim.102
  96.7 2.9 fusion.97
  99.5 3.4 fusion.98
  106.1 1.6 broadcast_in_dim.102
  108.9 2.9 fusion.97
  111.8 3.4 fusion.98
  118.4 1.6 broadcast_in_dim.102
  121.2 2.9 fusion.97
  124.1 3.4 fusion.98
  130.6 1.6 broadcast_in_dim.102
  133.4 2.9 fusion.97
  136.3 3.4 fusion.98
  142.9 1.6 broadcast_in_dim.102
  145.7 2.9 fusion.97
  148.6 3.4 fusion.98
  155.2 1.6 broadcast_in_dim.102
  158.0 2.9 fusion.97
  160.8 3.4 fusion.98
  167.4 1.6 broadcast_in_dim.102
  170.2 2.9 fusion.97
  173.1 3.4 fusion.98
  179.7 1.6 broadcast_in_dim.102
  182.5 2.9 fusion.97
  185.4 3.4 fusion.98
  191.9 1.6 broadcast_in_dim.102
  194.8 2.9 fusion.97
  197.6 3.4 fusion.98
  204.2 1.6 broadcast_in_dim.102
  207.0 2.9 fusion.97
  209.9 3.4 fusion.98
  213.3 1.4 fusion.100
  216.5 1.6 broadcast_in_dim.102
  219.3 2.9 fusion.97
  222.2 3.4 fusion.98
  228.7 1.6 broadcast_in_dim.102
  231.6 2.9 fusion.97
  234.4 3.4 fusion.98
  241.0 1.6 broadcast_in_dim.102
  243.8 2.9 fusion.97
  246.7 3.4 fusion.98
  250.1 1.4 fusion.100
  253.3 1.6 broadcast_in_dim.102
  256.1 2.9 fusion.97
  259.0 3.4 fusion.98
  265.5 1.6 broadcast_in_dim.102
  268.3 2.9 fusion.97
  271.2 3.4 fusion.98
  276.1 2.1 fusion.21
  278.3 76.4 %reduce-scatter.3.cloned.1.call-done = bf16[256,512]{0,1:T(8,128)(2,1)} async-done(((bf16[2048,512]{0,1:T(8,128)(2,1)}), bf16[256,512]{0,1:T(8,128)(2,1)}) %reduce-scatter.3.cloned.1.call-update) | async-done | bytes 262160 | tf_op jit(solution)/shard_map/reduce_scatter | solution.py:115
  358.4 3.5 collective-permute-done.1
  362.0 2.3 add_convert_fusion.1
  364.6 31.3 %all_to_all.5 = bf16[8,256,512]{2,1,0:T(8,128)(2,1)S(1)} all-to-all(bf16[8,256,512]{2,1,0:T(8,128)(2,1)S(1)} %stack.11), channel_id=1, replica_groups=mesh['seq'=16,'head'=8] {'head'}, dimensions={0} | all-to-all | bytes 4194304 | tf_op jit(solution)/shard_map/all_to_all | solution.py:134
  397.5 9.6 %fusion.22 = bf16[2048,512]{0,1:T(8,128)(2,1)} fusion(bf16[1024,2048]{1,0:T(8,128)(2,1)} %param.23, bf16[2048,512]{1,0:T(8,128)(2,1)S(1)} %fusion.20, bf16[2048,1024]{1,0:T(8,128)(2,1)} %param.22), kind=kOutput, calls=%fused_computation.40 | convolution fusion | flops 4298637312 | bytes 12582912 | tf_op jit(solution)/shard_map/fk,kc->cf/dot_general | solution.py:144
  407.1 76.2 %reduce-scatter.5.cloned.1.call-done = bf16[256,512]{0,1:T(8,128)(2,1)} async-done(((bf16[2048,512]{0,1:T(8,128)(2,1)}), bf16[256,512]{0,1:T(8,128)(2,1)}) %reduce-scatter.5.cloned.1.call-update) | async-done | bytes 262160 | tf_op jit(solution)/shard_map/reduce_scatter | solution.py:143
  483.4 1.7 fusion.58
  (233 shorter events, 73.9 us)
Async XLA Ops:
  6.5 269.6 %copy-start = (bf16[256,2048]{1,0:T(8,128)(2,1)S(1)}, bf16[256,2048]{1,0:T(8,128)(2,1)}, u32[]{:S(2)}) copy-start(bf16[256,2048]{1,0:T(8,128)(2,1)} %param.18) | copy-start | bytes 3145732
  6.5 6.3 %copy-start.7 = (s32[4]{0:T(128)S(1)}, s32[4]{0:T(128)}, u32[]{:S(2)}) copy-start(s32[4]{0:T(128)} %param.25) | copy-start | bytes 52
  6.5 6.4 %copy-start.4 = (s32[4,8]{1,0:T(4,128)S(1)}, s32[4,8]{1,0:T(4,128)}, u32[]{:S(2)}) copy-start(s32[4,8]{1,0:T(4,128)} %param.24) | copy-start | bytes 388
  6.5 6.5 %copy-start.6 = (bf16[2048,256]{1,0:T(8,128)(2,1)S(1)}, bf16[2048,256]{1,0:T(8,128)(2,1)}, u32[]{:S(2)}) copy-start(bf16[2048,256]{1,0:T(8,128)(2,1)} %param.15) | copy-start | bytes 3145732
  6.5 61.0 %all-gather.2.cloned.1.call-start = ((), (), s32[]{:S(2)}) async-start(), calls=%async_computation.3 | async-start | bytes 8912896 | tf_op jit(solution)/shard_map/all_gather | solution.py:93
  12.7 342.0 %reduce-scatter.3.cloned.1.call-start = ((), (), s32[]{:S(2)}) async-start(), calls=%async_computation.4 | async-start | bytes 2359296 | tf_op jit(solution)/shard_map/reduce_scatter | solution.py:115
  87.2 3.4 copy-start.1
  99.5 3.4 copy-start.1
  111.8 3.4 copy-start.1
  124.0 3.4 copy-start.1
  136.3 3.4 copy-start.1
  148.6 3.4 copy-start.1
  160.8 3.4 copy-start.1
  173.1 3.4 copy-start.1
  185.4 3.4 copy-start.1
  197.6 3.4 copy-start.1
  209.9 3.4 copy-start.1
  222.2 3.4 copy-start.1
  234.4 3.4 copy-start.1
  246.7 3.4 copy-start.1
  258.9 3.4 copy-start.1
  271.2 3.4 copy-start.1
  276.0 2.3 copy-start.2
  276.1 85.8 %copy-start.5 = (f32[256]{0:T(256)S(1)}, f32[256]{0:T(256)}, u32[]{:S(2)}) copy-start(f32[256]{0:T(256)} %param.20) | copy-start | bytes 3076
  278.3 205.1 %reduce-scatter.5.cloned.1.call-start = ((), (), s32[]{:S(2)}) async-start(), calls=%async_computation.5 | async-start | bytes 2359296 | tf_op jit(solution)/shard_map/reduce_scatter | solution.py:143
  355.8 2.6 collective-permute-start
  357.1 4.8 collective-permute-start.1
  364.6 32.3 %copy-start.3 = (f32[2048]{0:T(1024)S(1)}, f32[2048]{0:T(1024)}, u32[]{:S(2)}) copy-start(f32[2048]{0:T(1024)} %param.21) | copy-start | bytes 24580
Sparse Core Ops, SparseCore 0:
  12.8 54.6 all-gather.1
  278.4 76.2 reduce-scatter.2
  407.2 76.0 reduce-scatter.4
